TPU v7x, 256 devices: a whole 4x4x8 slice. The times are simulated.
256 devices in a mesh: frame: 8 (over z), tile: 32 (over x, y, core).
Axes of the slice: x: 4, y: 4, z: 8, core: 2. Of those that a mesh axis runs over, the one named last changes fastest.
Arguments:
- displacement: bfloat16 [512, 2, 32, 4096], P('frame', None, 'tile'), may hold values from -256 to 256
Outputs:
- basis: bfloat16 [512, 3, 32, 4096], P(None, None, 'tile', 'frame')
- factor: float32 [512, 512], replicated
All inputs are finite; a program needn't handle non-finite values.
Results may differ from a plain program's by a relative error of at most 0.0053.
The roundings to bfloat16 on the way count: a program that leaves them out, or rounds other values in their place, can miss the bound.
Values may be sent and summed in bfloat16 or wider, within the bound.
No kernel may reach another device: no remote copies, remote signals or barrier semaphores. Data moves between devices by JAX's collectives and lax.ppermute only.
A program may use at most 64 MiB of HBM per device.

v0:
```python
import math
import jax
import jax.numpy as jnp
from jax import lax
from jax.sharding import PartitionSpec as P


def with_halo(array, sides, width):
    for axis, dim in sides:
        peers, length = (lax.axis_size(axis), array.shape[dim])
        up = [(i, (i + 1) % peers) for i in range(peers - 1)]
        down = [(j, i) for i, j in up]
        last = lax.slice_in_dim(array, length - width, length, axis=dim)
        first = lax.slice_in_dim(array, 0, width, axis=dim)
        before = lax.ppermute(last, axis, up)
        after = lax.ppermute(first, axis, down)
        array = jnp.concatenate([before, array, after], axis=dim)
    return array


def derivative(center, before, after, first, final):
    return jnp.where(
        first, after - center, jnp.where(final, center - before, (after - before) * 0.5)
    )


def column_derivative(center):
    width = center.shape[-1]
    after = jnp.concatenate([center[..., 1:], center[..., -1:]], axis=-1)
    before = jnp.concatenate([center[..., :1], center[..., :-1]], axis=-1)
    column = jnp.arange(width, dtype=jnp.int32)
    return derivative(center, before, after, column == 0, column == width - 1)


def combine_strain(d_rows, d_cols):
    return jnp.stack(
        [d_cols[:, 0], d_rows[:, 1], 0.5 * (d_rows[:, 0] + d_cols[:, 1])], axis=1
    ).astype(jnp.bfloat16)


def local(displacement):
    rows = displacement.shape[2]
    full_width = displacement.shape[3]
    total_rows = lax.axis_size("tile") * rows
    scale = math.sqrt(3 * total_rows * full_width)
    row_global = lax.axis_index("tile") * rows + jnp.arange(rows, dtype=jnp.int32)
    first = (row_global == 0)[:, None]
    final = (row_global == total_rows - 1)[:, None]
    padded = with_halo(displacement, (("tile", 2),), 1)
    field = padded.astype(jnp.float32)
    center = field[:, :, 1:-1, :]
    d_rows = derivative(center, field[:, :, :-2, :], field[:, :, 2:, :], first, final)
    d_cols = column_derivative(center)
    strain = combine_strain(d_rows, d_cols)
    pixel_major = lax.all_to_all(strain, "frame", split_axis=3, concat_axis=0, tiled=True)
    frames = pixel_major.shape[0]
    snapshot_half = pixel_major.reshape(frames, -1)
    local_gram = lax.dot_general(
        snapshot_half, snapshot_half, (((1,), (1,)), ((), ())), preferred_element_type=jnp.float32
    )
    gram = lax.psum(local_gram, ("frame", "tile"))
    lower = jnp.linalg.cholesky(gram)
    snapshot = snapshot_half.astype(jnp.float32)
    solved = lax.linalg.triangular_solve(lower, snapshot, left_side=True, lower=True)
    basis = (solved * scale).astype(jnp.bfloat16).reshape(pixel_major.shape)
    return (basis, lower.T / scale)


def solution(mesh):
    return jax.shard_map(
        local,
        mesh=mesh,
        in_specs=(P("frame", None, "tile", None),),
        out_specs=(P(None, None, "tile", "frame"), P()),
        check_vma=False,
    )
```

profile of v0, /device:TPU:2, one launch (start us, length us, event | category | flops | bytes accessed | tf_op | source)
XLA Modules:
  0.0 526.9 jit_solution(18431249091505621572)
XLA Ops:
  7.2 1.8 copy.46
  9.0 1.9 collective-permute-start
  10.9 5.8 %collective-permute-start.1 = (bf16[64,2,1,4096]{3,0,2,1:T(8,128)(2,1)S(1)}, bf16[64,2,1,4096]{3,0,2,1:T(8,128)(2,1)S(1)}, u32[]{:S(2)}, u32[]{:S(2)}) collective-permute-start(bf16[64,2,1,4096]{3,0,2,1:T(8,128)(2,1)S(1)} %copy.46), channel_id=1, source_target_pairs={{1,0},{2,1},{3,2},{4,3},{5,4},{6,5},{7,6},{8,7},{9,8},{10,9},{11,1... | collective-permute-start | bytes 3145736 | tf_op jit(solution)/shard_map/ppermute | solution.py:16
  16.7 10.5 %collective-permute-done = bf16[64,2,1,4096]{3,0,2,1:T(8,128)(2,1)S(1)} collective-permute-done((bf16[64,2,1,4096]{3,0,2,1:T(8,128)(2,1)S(1)}, bf16[64,2,1,4096]{3,0,2,1:T(8,128)(2,1)S(1)}, u32[]{:S(2)}, u32[]{:S(2)}) %collective-permute-start) | collective-permute-done | bytes 1048608 | tf_op jit(solution)/shard_map/ppermute | solution.py:15
  27.2 1.8 collective-permute-done.1
  29.0 0.5 maximum_convert_fusion
  29.5 0.7 fusion.35
  30.3 1.5 select_select_fusion
  32.2 4.7 copy.49
  36.9 6.1 %reshape.243 = bf16[8,2,49152]{2,1,0:T(2,128)(2,1)S(1)} reshape(bf16[4096,1,3,64]{3,2,1,0:T(4,128)(2,1)} %bitcast.77) | data formatting | bytes 3145728
  43.0 48.1 %all_to_all.15 = bf16[8,2,49152]{2,1,0:T(2,128)(2,1)S(1)} all-to-all(bf16[8,2,49152]{2,1,0:T(2,128)(2,1)S(1)} %reshape.243), channel_id=1, replica_groups=mesh['frame'=8,'tile'=32] {'frame'}, dimensions={0} | all-to-all | bytes 3145728 | tf_op jit(solution)/shard_map/all_to_all | solution.py:55
  91.2 4.8 reshape.244
  96.0 4.8 copy.67
  100.8 1.4 copy.51
  102.1 0.5 copy.69
  102.7 2.0 fusion.36
  104.9 2.1 convert_element_type.26
  107.0 0.3 copy.54
  107.3 0.8 copy.70
  108.2 248.2 %all-reduce.3.cloned.1.call-done = f32[512,512]{0,1:T(8,128)} async-done(((f32[512,512]{0,1:T(8,128)}), f32[512,512]{0,1:T(8,128)}) %all-reduce.3.cloned.1.call-update) | async-done | bytes 1048592 | tf_op jit(solution)/shard_map/psum | solution.py:61
  356.4 1.6 copy.53
  358.3 11.7 %cholesky.104 = f32[128,128]{1,0:T(8,128)S(1)} custom-call(f32[128,128]{1,0:T(8,128)S(1)} %cholesky.266), custom_call_target="Cholesky" | custom-call | tf_op jit(solution)/shard_map/jit(cholesky)/cholesky | solution.py:62
  370.2 9.8 %custom-call.30 = f32[1,128,128]{1,2,0:T(8,128)S(1)} custom-call(f32[1,128,128]{2,1,0:T(8,128)S(1)} %get-tuple-element.45), custom_call_target="InvertDiagBlocksLowerTriangular" | custom-call | tf_op jit(solution)/shard_map/jit(cholesky)/cholesky | solution.py:62
  380.0 0.3 constant_dynamic-update-slice_fusion.3
  380.4 0.3 convolution_subtract_fusion.3
  380.7 11.8 %cholesky.217 = f32[128,128]{1,0:T(8,128)S(1)} custom-call(f32[128,128]{1,0:T(8,128)S(1)} %cholesky.270), custom_call_target="Cholesky" | custom-call | tf_op jit(solution)/shard_map/jit(cholesky)/cholesky | solution.py:62
  392.6 0.6 compare_reduce_fusion.2
  393.2 0.6 compare_reduce_fusion.3
  393.8 9.8 %custom-call.31 = f32[1,128,128]{1,2,0:T(8,128)S(1)} custom-call(f32[1,128,128]{2,1,0:T(8,128)S(1)} %get-tuple-element.42), custom_call_target="InvertDiagBlocksLowerTriangular" | custom-call | tf_op jit(solution)/shard_map/jit(cholesky)/cholesky | solution.py:62
  403.6 0.3 convolution_dynamic-update-slice_fusion
  403.9 0.4 convolution_subtract_fusion.4
  404.3 11.7 %cholesky.238 = f32[128,128]{1,0:T(8,128)S(1)} custom-call(f32[128,128]{1,0:T(8,128)S(1)} %cholesky.275), custom_call_target="Cholesky" | custom-call | tf_op jit(solution)/shard_map/jit(cholesky)/cholesky | solution.py:62
  416.1 0.7 compare_reduce_fusion.1
  416.7 9.8 %custom-call.32 = f32[1,128,128]{1,2,0:T(8,128)S(1)} custom-call(f32[1,128,128]{2,1,0:T(8,128)S(1)} %get-tuple-element.39), custom_call_target="InvertDiagBlocksLowerTriangular" | custom-call | tf_op jit(solution)/shard_map/jit(cholesky)/cholesky | solution.py:62
  426.7 0.4 convolution_subtract_fusion.5
  427.1 11.9 %cholesky.255 = f32[128,128]{1,0:T(8,128)S(1)} custom-call(f32[128,128]{1,0:T(8,128)S(1)} %convolution_subtract_fusion.5), custom_call_target="Cholesky" | custom-call | tf_op jit(solution)/shard_map/jit(cholesky)/cholesky | solution.py:62
  439.1 0.7 compare_reduce_fusion
  442.3 0.3 multiply_bitcast_fusion
  442.6 10.0 %while.1 = (s32[]{:T(128)}, f32[512,512]{1,0:T(8,128)S(1)}, s32[4,2]{0,1:T(2,128)S(1)}, f32[4,128,128]{2,1,0:T(8,128)}, s32[]{:T(128)}) while((s32[]{:T(128)}, f32[512,512]{1,0:T(8,128)S(1)}, s32[4,2]{0,1:T(2,128)S(1)}, f32[4,128,128]{2,1,0:T(8,128)}, s32[]{:T(128)}) %tuple.39), condition=%wide.while_cond, body=%wide.while_body.sunk | while | flops 2 | bytes 132705 | solution.py:64
  442.7 0.5 fusion.46
  443.2 1.9 bitcast_dynamic-update-slice_fusion.2
  445.2 0.5 fusion.46
  445.7 1.9 bitcast_dynamic-update-slice_fusion.2
  447.7 0.5 fusion.46
  448.2 1.9 bitcast_dynamic-update-slice_fusion.2
  450.2 0.5 fusion.46
  450.7 1.9 bitcast_dynamic-update-slice_fusion.2
  452.6 40.2 %custom-call.33 = f32[4,128,128]{1,2,0:T(8,128)S(1)} custom-call(f32[4,128,128]{2,1,0:T(8,128)} %get-tuple-element.9), custom_call_target="InvertDiagBlocksLowerTriangular" | custom-call | tf_op jit(solution)/shard_map/triangular_solve | solution.py:64
  492.8 1.6 fusion.26
  494.4 2.1 convolution_subtract_fusion.2
  496.5 1.7 fusion.25
  498.3 1.9 convolution_subtract_fusion
  500.2 1.7 fusion.23
  501.9 3.4 fusion.1
  505.3 1.1 copy.57
  506.4 1.2 copy.56
  507.6 1.1 copy.55
  508.7 1.4 copy.58
  510.1 1.7 convolution_bitcast_fusion
  511.8 0.3 copy.62
  512.1 1.4 copy.61
  513.5 2.3 copy.60
  515.8 1.3 copy.64
  517.1 2.7 fusion.7
  (36 shorter events, 1.8 us)
Async XLA Ops:
  7.2 349.3 %all-reduce.3.cloned.1.call-start = ((), (), s32[]{:S(2)}) async-start(), calls=%async_computation.1 | async-start | bytes 2097152 | tf_op jit(solution)/shard_map/psum | solution.py:61
  9.0 18.2 %collective-permute-start = (bf16[64,2,1,4096]{3,0,2,1:T(8,128)(2,1)S(1)}, bf16[64,2,1,4096]{3,0,2,1:T(8,128)(2,1)S(1)}, u32[]{:S(2)}, u32[]{:S(2)}) collective-permute-start(bf16[64,2,1,4096]{3,0,2,1:T(8,128)(2,1)S(1)} %copy.46), channel_id=1, source_target_pairs={{0,1},{1,2},{2,3},{3,4},{4,5},{5,6},{6,7},{7,8},{8,9},{9,10},{10,1... | collective-permute-start | bytes 3145736 | tf_op jit(solution)/shard_map/ppermute | solution.py:15
  10.9 18.1 %collective-permute-start.1 = (bf16[64,2,1,4096]{3,0,2,1:T(8,128)(2,1)S(1)}, bf16[64,2,1,4096]{3,0,2,1:T(8,128)(2,1)S(1)}, u32[]{:S(2)}, u32[]{:S(2)}) collective-permute-start(bf16[64,2,1,4096]{3,0,2,1:T(8,128)(2,1)S(1)} %copy.46), channel_id=1, source_target_pairs={{1,0},{2,1},{3,2},{4,3},{5,4},{6,5},{7,6},{8,7},{9,8},{10,9},{11,1... | collective-permute-start | bytes 3145736 | tf_op jit(solution)/shard_map/ppermute | solution.py:16
  356.4 1.7 copy-start.1
  452.6 40.2 %copy-start.3 = (f32[512,512]{1,0:T(8,128)}, f32[512,512]{1,0:T(8,128)S(1)}, u32[]{:S(2)}) copy-start(f32[512,512]{1,0:T(8,128)S(1)} %get-tuple-element.100) | copy-start | bytes 3145732
  492.8 1.6 copy-start.4
  494.4 3.8 copy-start
  507.6 4.3 copy-start.2
Sparse Core Ops, SparseCore 0:
  104.8 251.5 all-reduce.2
where the time goes:
time: 532 us; the launch traced here: 527 us
  waiting for transfers between devices  261 us (49%)
  other arithmetic  127 us (24%)
  local copies, waits for them, and re-layouts  48.3 us (9%)
  blocking collectives  48.1 us (9%)
  matrix products  17.9 us (3%)
  between operations  17.2 us (3%)
  starting transfers between devices  7.71 us (1%)
    psum x1, waiting for transfers between devices, local(): gram = lax.psum(local_gram, ('frame', 'tile'))  248 us
    another operation x15, other arithmetic, local(): lower = jnp.linalg.cholesky(gram)  79.4 us
    all_to_all x1, blocking collectives, local(): lax.all_to_all(strain, 'frame', split_axis=3, concat_axis=0, tiled=True)  48.1 us
    another operation x2, other arithmetic, local(): lax.linalg.triangular_solve(lower, snapshot, left_side=True, lower=True)  40.2 us
    unnamed x16, local copies, waits for them, and re-layouts  15.4 us
    another operation x7, matrix products, local(): lax.linalg.triangular_solve(lower, snapshot, left_side=True, lower=True)  14.1 us
  transfers between devices with their start and end apart: 3, of which 3 were waited for; matrix products, arithmetic and copies ran while one was open for 1% of the time, Pallas kernels for 0%

commit v1 on v0

--- a/solution.py
+++ b/solution.py
@@ -1,8 +1,17 @@
+import functools
 import math
 import jax
 import jax.numpy as jnp
 from jax import lax
 from jax.sharding import PartitionSpec as P
+from jax.lax import psum
+
+
+def change_roads_up(slab_in, group_axis, axis_id):
+    return psum(psum(slab_in, group_axis), axis_id)
+
+
+begin_seats_all_on = functools.partial(change_roads_up, group_axis="frame", axis_id="tile")
 
 
 def with_halo(array, sides, width):
@@ -58,7 +67,7 @@
     local_gram = lax.dot_general(
         snapshot_half, snapshot_half, (((1,), (1,)), ((), ())), preferred_element_type=jnp.float32
     )
-    gram = lax.psum(local_gram, ("frame", "tile"))
+    gram = begin_seats_all_on(local_gram)
     lower = jnp.linalg.cholesky(gram)
     snapshot = snapshot_half.astype(jnp.float32)
     solved = lax.linalg.triangular_solve(lower, snapshot, left_side=True, lower=True)

time: 532 us -> 471 us (0.89)
  waiting for transfers between devices: 261 us -> 196 us
    psum x1 -> x2, waiting for transfers between devices: 248 us -> 184 us  [change_roads_up(): return psum(psum(slab_in, group_axis), axis_id)]
  transfers between devices with their start and end apart: 3 -> 4, of which waited for: 3 -> 4; matrix products, arithmetic and copies ran while one was open for 1% -> 1% of each run, Pallas kernels for 0% -> 0%
where the time goes in v1:
time: 471 us; the launch traced here: 462 us
  waiting for transfers between devices  196 us (42%)
  other arithmetic  127 us (27%)
  blocking collectives  48.1 us (10%)
  local copies, waits for them, and re-layouts  47.8 us (10%)
  matrix products  17.9 us (4%)
  between operations  17.2 us (4%)
  starting transfers between devices  8.22 us (2%)
    psum x2, waiting for transfers between devices, change_roads_up(): return psum(psum(slab_in, group_axis), axis_id)  184 us
    another operation x15, other arithmetic, local(): lower = jnp.linalg.cholesky(gram)  79.4 us
    all_to_all x1, blocking collectives, local(): lax.all_to_all(strain, 'frame', split_axis=3, concat_axis=0, tiled=True)  48.1 us
    another operation x2, other arithmetic, local(): lax.linalg.triangular_solve(lower, snapshot, left_side=True, lower=True)  40.2 us
    unnamed x16, local copies, waits for them, and re-layouts  15.4 us
    another operation x7, matrix products, local(): lax.linalg.triangular_solve(lower, snapshot, left_side=True, lower=True)  14.1 us
    ppermute x1, waiting for transfers between devices, with_halo(): before = lax.ppermute(last, axis, up)  10.5 us
    another operation x12, local copies, waits for them, and re-layouts  9.98 us
  transfers between devices with their start and end apart: 4, of which 4 were waited for; matrix products, arithmetic and copies ran while one was open for 1% of the time, Pallas kernels for 0%

profile of v1, /device:TPU:2, one launch (start us, length us, event | category | flops | bytes accessed | tf_op | source)
XLA Modules:
  0.0 462.4 jit_solution(18407480531897664892)
XLA Ops:
  7.2 1.8 copy.46
  9.0 1.9 collective-permute-start
  10.9 5.8 %collective-permute-start.1 = (bf16[64,2,1,4096]{3,0,2,1:T(8,128)(2,1)S(1)}, bf16[64,2,1,4096]{3,0,2,1:T(8,128)(2,1)S(1)}, u32[]{:S(2)}, u32[]{:S(2)}) collective-permute-start(bf16[64,2,1,4096]{3,0,2,1:T(8,128)(2,1)S(1)} %copy.46), channel_id=1, source_target_pairs={{1,0},{2,1},{3,2},{4,3},{5,4},{6,5},{7,6},{8,7},{9,8},{10,9},{11,1... | collective-permute-start | bytes 3145736 | tf_op jit(solution)/shard_map/ppermute | solution.py:25
  16.7 10.5 %collective-permute-done = bf16[64,2,1,4096]{3,0,2,1:T(8,128)(2,1)S(1)} collective-permute-done((bf16[64,2,1,4096]{3,0,2,1:T(8,128)(2,1)S(1)}, bf16[64,2,1,4096]{3,0,2,1:T(8,128)(2,1)S(1)}, u32[]{:S(2)}, u32[]{:S(2)}) %collective-permute-start) | collective-permute-done | bytes 1048608 | tf_op jit(solution)/shard_map/ppermute | solution.py:24
  27.2 1.8 collective-permute-done.1
  29.0 0.5 maximum_convert_fusion
  29.5 0.7 fusion.35
  30.3 1.5 select_select_fusion
  32.2 4.7 %copy.49 = bf16[64,3,1,4096]{0,1,2,3:T(4,128)(2,1)} copy(bf16[64,3,1,4096]{3,0,2,1:T(8,128)(2,1)S(1)} %pad_maximum_fusion.2) | data formatting | bytes 3145728 | tf_op jit(solution)/shard_map/stack | solution.py:45
  36.9 6.1 %reshape.243 = bf16[8,2,49152]{2,1,0:T(2,128)(2,1)S(1)} reshape(bf16[4096,1,3,64]{3,2,1,0:T(4,128)(2,1)} %bitcast.77) | data formatting | bytes 3145728
  43.0 48.1 %all_to_all.15 = bf16[8,2,49152]{2,1,0:T(2,128)(2,1)S(1)} all-to-all(bf16[8,2,49152]{2,1,0:T(2,128)(2,1)S(1)} %reshape.243), channel_id=1, replica_groups=mesh['frame'=8,'tile'=32] {'frame'}, dimensions={0} | all-to-all | bytes 3145728 | tf_op jit(solution)/shard_map/all_to_all | solution.py:64
  91.2 4.8 %reshape.244 = bf16[4096,1,3,64]{3,2,1,0:T(4,128)(2,1)} reshape(bf16[8,2,49152]{2,1,0:T(2,128)(2,1)S(1)} %all_to_all.15) | data formatting | bytes 3145728
  96.0 4.3 copy.67
  100.3 1.4 copy.51
  101.7 0.5 copy.69
  102.2 2.0 fusion.36
  104.2 0.5 all-reduce.6.cloned.1.call-start
  104.7 71.2 %all-reduce.4.cloned.1.call-done = f32[512,512]{0,1:T(8,128)} async-done(((f32[512,512]{0,1:T(8,128)}), f32[512,512]{0,1:T(8,128)}) %all-reduce.4.cloned.1.call-update) | async-done | bytes 1048592 | tf_op jit(solution)/shard_map/psum | solution.py:11
  176.2 2.1 convert_element_type.26
  178.3 0.3 copy.54
  178.6 0.8 copy.70
  179.4 112.5 %all-reduce.6.cloned.1.call-done = f32[512,512]{0,1:T(8,128)} async-done(((f32[512,512]{0,1:T(8,128)}), f32[512,512]{0,1:T(8,128)}) %all-reduce.6.cloned.1.call-update) | async-done | bytes 1048592 | tf_op jit(solution)/shard_map/psum | solution.py:11
  291.9 1.6 copy.53
  293.8 11.7 %cholesky.104 = f32[128,128]{1,0:T(8,128)S(1)} custom-call(f32[128,128]{1,0:T(8,128)S(1)} %cholesky.266), custom_call_target="Cholesky" | custom-call | tf_op jit(solution)/shard_map/jit(cholesky)/cholesky | solution.py:71
  305.7 9.8 %custom-call.30 = f32[1,128,128]{1,2,0:T(8,128)S(1)} custom-call(f32[1,128,128]{2,1,0:T(8,128)S(1)} %get-tuple-element.45), custom_call_target="InvertDiagBlocksLowerTriangular" | custom-call | tf_op jit(solution)/shard_map/jit(cholesky)/cholesky | solution.py:71
  315.5 0.3 constant_dynamic-update-slice_fusion.3
  315.9 0.3 convolution_subtract_fusion.3
  316.2 11.7 %cholesky.217 = f32[128,128]{1,0:T(8,128)S(1)} custom-call(f32[128,128]{1,0:T(8,128)S(1)} %cholesky.270), custom_call_target="Cholesky" | custom-call | tf_op jit(solution)/shard_map/jit(cholesky)/cholesky | solution.py:71
  328.0 0.6 compare_reduce_fusion.2
  328.6 0.6 compare_reduce_fusion.3
  329.2 10.0 %custom-call.31 = f32[1,128,128]{1,2,0:T(8,128)S(1)} custom-call(f32[1,128,128]{2,1,0:T(8,128)S(1)} %get-tuple-element.42), custom_call_target="InvertDiagBlocksLowerTriangular" | custom-call | tf_op jit(solution)/shard_map/jit(cholesky)/cholesky | solution.py:71
  339.4 0.4 convolution_subtract_fusion.4
  339.8 11.7 %cholesky.238 = f32[128,128]{1,0:T(8,128)S(1)} custom-call(f32[128,128]{1,0:T(8,128)S(1)} %cholesky.275), custom_call_target="Cholesky" | custom-call | tf_op jit(solution)/shard_map/jit(cholesky)/cholesky | solution.py:71
  351.6 0.7 compare_reduce_fusion.1
  352.2 9.8 %custom-call.32 = f32[1,128,128]{1,2,0:T(8,128)S(1)} custom-call(f32[1,128,128]{2,1,0:T(8,128)S(1)} %get-tuple-element.39), custom_call_target="InvertDiagBlocksLowerTriangular" | custom-call | tf_op jit(solution)/shard_map/jit(cholesky)/cholesky | solution.py:71
  362.2 0.4 convolution_subtract_fusion.5
  362.6 11.9 %cholesky.255 = f32[128,128]{1,0:T(8,128)S(1)} custom-call(f32[128,128]{1,0:T(8,128)S(1)} %convolution_subtract_fusion.5), custom_call_target="Cholesky" | custom-call | tf_op jit(solution)/shard_map/jit(cholesky)/cholesky | solution.py:71
  374.6 0.7 compare_reduce_fusion
  377.8 0.3 multiply_bitcast_fusion
  378.1 10.0 %while.1 = (s32[]{:T(128)}, f32[512,512]{1,0:T(8,128)S(1)}, s32[4,2]{0,1:T(2,128)S(1)}, f32[4,128,128]{2,1,0:T(8,128)}, s32[]{:T(128)}) while((s32[]{:T(128)}, f32[512,512]{1,0:T(8,128)S(1)}, s32[4,2]{0,1:T(2,128)S(1)}, f32[4,128,128]{2,1,0:T(8,128)}, s32[]{:T(128)}) %tuple.39), condition=%wide.while_cond, body=%wide.while_body.sunk | while | flops 2 | bytes 132705 | solution.py:73
  378.2 0.5 fusion.46
  378.7 1.9 bitcast_dynamic-update-slice_fusion.2
  380.7 0.5 fusion.46
  381.2 1.9 bitcast_dynamic-update-slice_fusion.2
  383.2 0.5 fusion.46
  383.7 1.9 bitcast_dynamic-update-slice_fusion.2
  385.7 0.5 fusion.46
  386.2 1.9 bitcast_dynamic-update-slice_fusion.2
  388.1 40.2 %custom-call.33 = f32[4,128,128]{1,2,0:T(8,128)S(1)} custom-call(f32[4,128,128]{2,1,0:T(8,128)} %get-tuple-element.9), custom_call_target="InvertDiagBlocksLowerTriangular" | custom-call | tf_op jit(solution)/shard_map/triangular_solve | solution.py:73
  428.3 1.6 fusion.26
  429.9 2.1 convolution_subtract_fusion.2
  432.0 1.7 fusion.25
  433.7 1.9 convolution_subtract_fusion
  435.7 1.7 fusion.23
  437.4 3.4 fusion.1
  440.8 1.1 copy.57
  441.9 1.2 copy.56
  443.1 1.1 copy.55
  444.2 1.4 copy.58
  445.6 1.7 convolution_bitcast_fusion
  447.6 1.4 copy.61
  449.0 2.3 copy.60
  451.3 1.3 copy.64
  452.6 2.7 fusion.7
  (39 shorter events, 2.3 us)
Async XLA Ops:
  7.2 168.8 %all-reduce.4.cloned.1.call-start = ((), (), s32[]{:S(2)}) async-start(), calls=%async_computation.1 | async-start | bytes 2097152 | tf_op jit(solution)/shard_map/psum | solution.py:11
  9.0 18.2 %collective-permute-start = (bf16[64,2,1,4096]{3,0,2,1:T(8,128)(2,1)S(1)}, bf16[64,2,1,4096]{3,0,2,1:T(8,128)(2,1)S(1)}, u32[]{:S(2)}, u32[]{:S(2)}) collective-permute-start(bf16[64,2,1,4096]{3,0,2,1:T(8,128)(2,1)S(1)} %copy.46), channel_id=1, source_target_pairs={{0,1},{1,2},{2,3},{3,4},{4,5},{5,6},{6,7},{7,8},{8,9},{9,10},{10,1... | collective-permute-start | bytes 3145736 | tf_op jit(solution)/shard_map/ppermute | solution.py:24
  10.9 18.1 %collective-permute-start.1 = (bf16[64,2,1,4096]{3,0,2,1:T(8,128)(2,1)S(1)}, bf16[64,2,1,4096]{3,0,2,1:T(8,128)(2,1)S(1)}, u32[]{:S(2)}, u32[]{:S(2)}) collective-permute-start(bf16[64,2,1,4096]{3,0,2,1:T(8,128)(2,1)S(1)} %copy.46), channel_id=1, source_target_pairs={{1,0},{2,1},{3,2},{4,3},{5,4},{6,5},{7,6},{8,7},{9,8},{10,9},{11,1... | collective-permute-start | bytes 3145736 | tf_op jit(solution)/shard_map/ppermute | solution.py:25
  104.2 187.7 %all-reduce.6.cloned.1.call-start = ((), (), s32[]{:S(2)}) async-start(), calls=%async_computation.2 | async-start | bytes 2097152 | tf_op jit(solution)/shard_map/psum | solution.py:11
  291.9 1.7 copy-start.1
  388.1 40.2 %copy-start.3 = (f32[512,512]{1,0:T(8,128)}, f32[512,512]{1,0:T(8,128)S(1)}, u32[]{:S(2)}) copy-start(f32[512,512]{1,0:T(8,128)S(1)} %get-tuple-element.101) | copy-start | bytes 3145732
  428.3 1.6 copy-start.4
  429.9 3.8 copy-start
  443.1 4.3 copy-start.2
Sparse Core Ops, SparseCore 0:
  104.3 71.5 all-reduce.3
  179.1 112.7 all-reduce.5
